TPU v7x, 32 devices: a whole 2x2x4 slice. The times are simulated.
32 devices in a mesh: gx: 8 (over z, x), gy: 4 (over y, core).
Axes of the slice: x: 2, y: 2, z: 4, core: 2. Of those that a mesh axis runs over, the one named last changes fastest.
Arguments:
- field: float32 [20, 64, 64, 256], P(None, 'gx', 'gy'), may hold values from -6 to 6
- spectral_weight: float32 [3, 2, 20, 20, 16, 64, 32], P(None, None, None, None, 'gx', 'gy'), may hold values from -12 to 12
- point_weight: float32 [3, 20, 20], replicated, may hold values from -1.25 to 1.25
- bias: float32 [3, 20], replicated, may hold values from -3 to 3
Outputs:
- result: float32 [20, 64, 64, 256], P(None, 'gx', 'gy')
All inputs are finite; a program needn't handle non-finite values.
Results may differ from a plain program's by a relative error of at most 0.00011.
Values sent between devices are 32-bit elements; how exact they have to be, the bound alone decides.
No kernel may reach another device: no remote copies, remote signals or barrier semaphores. Data moves between devices by JAX's collectives and lax.ppermute only.
A program may use at most 192 MiB of HBM per device.

v0:
```python
import jax
import jax.numpy as jnp
from jax import lax
from jax.sharding import PartitionSpec as P

NZ = 256
MZ = 16
MX = 64
MY = 32
LAYERS = 3


highest = lax.Precision.HIGHEST


def mode_list(count, points):
    half = count // 2
    lower = jnp.arange(half, dtype=jnp.int32)
    return jnp.concatenate([lower, points - half + lower])


def angles(modes, points):
    grid = jnp.arange(points, dtype=jnp.int32)
    product = grid[:, None] * modes[None, :] % points
    return 2.0 * jnp.pi / points * product.astype(jnp.float32)


def forward_table(modes, points):
    phase = angles(modes, points)
    cosine, sine = (jnp.cos(phase), jnp.sin(phase))
    return jnp.stack([jnp.stack([cosine, -sine], -1), jnp.stack([sine, cosine], -1)], 1)


def inverse_table(modes, points):
    phase = angles(modes, points).T
    cosine, sine = (jnp.cos(phase), jnp.sin(phase))
    return jnp.stack([jnp.stack([cosine, sine], -1), jnp.stack([-sine, cosine], -1)], 0)


def time_tables(total):
    modes = jnp.arange(MZ, dtype=jnp.int32)
    phase = angles(modes, NZ)
    forward = jnp.stack([jnp.cos(phase), -jnp.sin(phase)], -1)
    weight_k = jnp.where(modes == 0, 1.0, 2.0).astype(jnp.float32) / total
    inverse = jnp.stack([jnp.cos(phase).T, -jnp.sin(phase).T], 1) * weight_k[:, None, None]
    return (forward, inverse)


def mix_modes(spectrum, weights):
    shape = spectrum.shape
    flat = spectrum.reshape(2, shape[1], -1)
    kernel = weights.reshape(2, shape[1], shape[1], -1)

    def paired(left, right):
        return jnp.einsum("cm,com->om", left, right, precision=highest)

    real_part = paired(flat[0], kernel[0]) - paired(flat[1], kernel[1])
    imag_part = paired(flat[0], kernel[1]) + paired(flat[1], kernel[0])
    return jnp.stack([real_part, imag_part]).reshape(shape)


def shards(field, spectral_weight, point_weight, bias):
    channels, rows_x, rows_y, depth_z = field.shape
    count_x = lax.axis_size("gx")
    count_y = lax.axis_size("gy")
    points_x = rows_x * count_x
    points_y = rows_y * count_y
    local_z = MZ // count_x
    local_x = MX // count_y
    kx_modes = mode_list(MX, points_x)
    ky_modes = mode_list(MY, points_y)
    table_z, inv_z = time_tables(float(points_x * points_y * depth_z))
    table_x = forward_table(kx_modes, points_x).reshape(points_x, 2, 2 * MX)
    table_y = forward_table(ky_modes, points_y).transpose(0, 1, 3, 2)
    inv_x = inverse_table(kx_modes, points_x).transpose(1, 0, 2, 3).reshape(2 * MX, points_x, 2)
    inv_y = inverse_table(ky_modes, points_y)
    current = field
    for layer_index in range(LAYERS):
        spectrum = jnp.einsum("cxyz,zkp->kxpcy", current, table_z, precision=highest).reshape(
            MZ, rows_x, -1
        )
        spectrum = lax.all_to_all(spectrum, "gx", split_axis=0, concat_axis=1, tiled=True)
        spectrum = spectrum.reshape(local_z, points_x, 2, channels, rows_y)
        spectrum = jnp.einsum("kxpcy,xpm->kcym", spectrum, table_x, precision=highest)
        spectrum = lax.all_to_all(spectrum, "gy", split_axis=3, concat_axis=2, tiled=True)
        spectrum = spectrum.reshape(local_z, channels, points_y, local_x, 2)
        spectrum = jnp.einsum("kcyxp,ypqj->qckxj", spectrum, table_y, precision=highest)
        mixed = mix_modes(spectrum, spectral_weight[layer_index])
        lines = jnp.einsum("pokxj,pjyq->koyxq", mixed, inv_y, precision=highest)
        lines = lines.reshape(local_z, channels, points_y, 2 * local_x)
        lines = lax.all_to_all(lines, "gy", split_axis=2, concat_axis=3, tiled=True)
        planes = jnp.einsum("kcym,mxq->kxqcy", lines, inv_x, precision=highest).reshape(
            local_z, points_x, -1
        )
        planes = lax.all_to_all(planes, "gx", split_axis=1, concat_axis=0, tiled=True).reshape(
            MZ, rows_x, 2, channels, rows_y
        )
        wave = jnp.einsum("kxpcy,kpz->cxyz", planes, inv_z, precision=highest)
        local = jnp.einsum("co,cxyz->oxyz", point_weight[layer_index], current, precision=highest)
        current = jax.nn.gelu(
            wave + local + bias[layer_index][:, None, None, None], approximate=False
        )
    return current


def solution(mesh):
    return jax.shard_map(
        shards,
        mesh=mesh,
        in_specs=(P(None, "gx", "gy", None), P(None, None, None, None, "gx", "gy", None), P(), P()),
        out_specs=P(None, "gx", "gy", None),
        check_vma=False,
    )
```

profile of v0, /device:TPU:0, one launch (start us, length us, event | category | flops | bytes accessed | tf_op | source)
XLA Modules:
  0.0 468.4 jit_solution(18149156900088146215)
XLA Ops:
  0.7 12.6 %fusion.48 = f32[16,8,2,20,16]{3,0,4,1,2:T(8,128)} fusion(f32[20,8,16,256]{3,2,1,0:T(8,128)} %param.4, f32[256,16,1]{0,1,2:T(8,128)S(1)} %get-tuple-element.60, f32[256,16,1]{0,1,2:T(8,128)S(1)} %get-tuple-element.61), kind=kOutput, calls=%fused_computation.89 | convolution fusion | flops 251666432 | bytes 2981888 | tf_op jit(solution)/shard_map/cxyz,zkp->kxpcy/dot_general | solution.py:79
  13.3 3.0 copy.296
  17.9 7.5 %all-to-all-start = ((f32[16,8,640]{2,1,0:T(8,128)}), f32[16,8,640]{2,1,0:T(8,128)S(1)}, u32[]{:S(2)}, u32[]{:S(2)}) async-start(f32[16,8,640]{2,1,0:T(8,128)} %reshape.741), calls=%async_computation | async-start | bytes 655360 | tf_op jit(solution)/shard_map/all_to_all | solution.py:82
  26.5 26.7 %fusion.152 = (f32[1,1,20,20,2,16,32]{6,5,4,3,2,1,0:T(8,128)}, f32[1,1,20,20,2,16,32]{6,5,4,3,2,1,0:T(8,128)}, f32[1,1,20,20,2,16,32]{6,5,4,3,2,1,0:T(8,128)}, f...) fusion(f32[3,2,20,20,2,16,32]{6,5,4,3,2,1,0:T(8,128)} %param.5), kind=kLoop, calls=%fused_computation.250 | loop fusion | bytes 19660800 | tf_op jit(solution)/shard_map/slice | solution.py:57
  56.4 4.4 fusion.50
  62.7 3.0 reshape.824
  65.7 3.7 all-to-all-start.1
  69.5 6.3 %squeeze.58 = f32[20,20,1024]{2,1,0:T(8,128)} reshape(f32[1,1,20,20,2,16,32]{6,5,4,3,2,1,0:T(8,128)} %get-tuple-element.27) | data formatting | bytes 3276800 | tf_op jit(solution)/shard_map/squeeze | solution.py:57
  75.8 6.4 %squeeze.60 = f32[20,20,1024]{2,1,0:T(8,128)} reshape(f32[1,1,20,20,2,16,32]{6,5,4,3,2,1,0:T(8,128)} %get-tuple-element.26) | data formatting | bytes 3276800 | tf_op jit(solution)/shard_map/squeeze | solution.py:57
  84.9 3.8 reshape.825
  88.7 3.8 copy.304
  103.4 3.5 all-to-all-start.2
  108.3 5.2 %all-to-all-done.2 = f32[4,1,20480]{2,1,0:T(1,128)S(1)} async-done(((f32[4,1,20480]{2,1,0:T(1,128)}), f32[4,1,20480]{2,1,0:T(1,128)S(1)}, u32[]{:S(2)}, u32[]{:S(2)}) %all-to-all-start.2) | async-done | bytes 327712 | tf_op jit(solution)/shard_map/all_to_all | solution.py:91
  122.0 6.2 %all-to-all-start.3 = ((f32[2,64,640]{2,0,1:T(2,128)}), f32[2,64,640]{2,0,1:T(2,128)S(1)}, u32[]{:S(2)}, u32[]{:S(2)}) async-start(f32[2,64,640]{2,0,1:T(2,128)} %copy.317), calls=%async_computation.3 | async-start | bytes 655360 | tf_op jit(solution)/shard_map/all_to_all | solution.py:95
  129.6 6.3 %fusion = f32[20,8,16,256]{3,0,2,1:T(8,128)} fusion(f32[20,8,16,256]{3,2,1,0:T(8,128)S(1)} %copy-done, f32[3,20,20]{2,1,0:T(8,128)} %param.6), kind=kOutput, calls=%fused_computation.3 | convolution fusion | flops 157286400 | bytes 5255168 | tf_op jit(solution)/shard_map/co,cxyz->oxyz/dot_general | solution.py:99
  135.9 2.3 all-to-all-done.3
  141.1 3.1 copy.320
  144.2 7.0 %fusion.49 = (u16[20,8,256]{2,0,1:T(8,128)(2,1)S(1)}, f32[20,8,16,256]{3,0,2,1:T(8,128)S(1)}) fusion(f32[20]{0:T(128)} %get-tuple-element.44, f32[20,8,16,256]{3,0,2,1:T(8,128)} %fusion, f32[16,8,2,20,16]{3,0,2,4,1:T(8,128)} %copy.320, f32[16,1,256]{2,0,1:T(8,128)S(1)} %copy-done.13, f32[16,1,256]{2,0,1:T(8,128)S(1)} %copy-done.15, f32[16]{0:T(128)} %fusion.136), kind=kOutput, calls=%fused_computation.90 | convolution fusion | flops 257531904 | bytes 5685392 | tf_op jit(solution)/shard_map/kxpcy,kpz->cxyz/dot_general | solution.py:98
  151.2 7.0 %fusion.4 = f32[20,8,16,256]{3,0,2,1:T(8,128)S(1)} fusion(f32[20,8,16,256]{3,0,2,1:T(8,128)S(1)} %get-tuple-element.59, u16[20,8,256]{2,0,1:T(8,128)(2,1)S(1)} %get-tuple-element.58), kind=kLoop, calls=%fused_computation.8 | loop fusion | flops 43909120 | bytes 5324800 | tf_op jit(solution)/shard_map/mul | solution.py:100
  158.3 10.5 %fusion.42 = f32[16,8,2,20,16]{3,0,4,1,2:T(8,128)} fusion(f32[20,8,16,256]{3,0,2,1:T(8,128)S(1)} %fusion.4, f32[256,16,1]{0,1,2:T(8,128)S(1)} %get-tuple-element.60, f32[256,16,1]{0,1,2:T(8,128)S(1)} %copy-done.12), kind=kOutput, calls=%fused_computation.87 | convolution fusion | flops 251666432 | bytes 2981888 | tf_op jit(solution)/shard_map/cxyz,zkp->kxpcy/dot_general | solution.py:79
  168.8 4.1 copy.323
  172.9 3.2 reshape.747
  176.1 14.5 %all_to_all.189 = f32[16,8,640]{2,1,0:T(8,128)S(1)} all-to-all(f32[16,8,640]{2,1,0:T(8,128)} %reshape.747), channel_id=1, replica_groups=mesh['gx'=8,'gy'=4] {'gx'}, dimensions={0} | all-to-all | bytes 655360 | tf_op jit(solution)/shard_map/all_to_all | solution.py:82
  191.3 3.3 reshape.748
  194.7 7.0 %fusion.53 = f32[2,20,16,128]{3,2,1,0:T(8,128)} fusion(f32[2,64,2,20,16]{4,3,2,1,0:T(8,128)} %reshape.748, f32[64,1,128]{2,0,1:T(8,128)S(1)} %copy.301, f32[64,1,128]{2,0,1:T(8,128)S(1)} %copy.300), kind=kOutput, calls=%fused_computation.101 | convolution fusion | flops 125845504 | bytes 720896 | tf_op jit(solution)/shard_map/kxpcy,xpm->kcym/dot_general | solution.py:84
  201.7 3.8 copy.326
  205.5 4.1 reshape.828
  209.7 4.3 all-to-all-start.5
  213.9 6.3 %squeeze.63 = f32[20,20,1024]{2,1,0:T(8,128)} reshape(f32[1,1,20,20,2,16,32]{6,5,4,3,2,1,0:T(8,128)} %get-tuple-element.25) | data formatting | bytes 3276800 | tf_op jit(solution)/shard_map/squeeze | solution.py:57
  220.2 6.3 %squeeze.65 = f32[20,20,1024]{2,1,0:T(8,128)} reshape(f32[1,1,20,20,2,16,32]{6,5,4,3,2,1,0:T(8,128)} %get-tuple-element.24) | data formatting | bytes 3276800 | tf_op jit(solution)/shard_map/squeeze | solution.py:57
  226.5 3.2 reduce.28
  229.7 4.7 %reshape.829 = f32[128,2,16,20]{3,2,1,0:T(8,128)} reshape(f32[4,20480]{1,0:T(4,128)} %reduce.28) | data formatting | bytes 655360
  234.4 4.7 %copy.327 = f32[2,20,16,4,32]{2,3,4,1,0:T(4,128)} copy(f32[2,20,16,4,32]{1,2,0,4,3:T(8,128)} %bitcast.387) | data formatting | bytes 655360 | tf_op jit(solution)/shard_map/all_to_all | solution.py:85
  239.1 3.9 reshape.749
  251.4 3.5 multiply_reduce_fusion.7
  264.0 2.3 copy.334
  266.3 3.3 reshape.830
  269.7 11.3 %all_to_all.190 = f32[4,1,20480]{2,1,0:T(1,128)} all-to-all(f32[4,1,20480]{2,1,0:T(1,128)} %reshape.830), channel_id=1, replica_groups=mesh['gx'=8,'gy'=4] {'gy'}, dimensions={0} | all-to-all | bytes 655360 | tf_op jit(solution)/shard_map/all_to_all | solution.py:91
  281.0 3.2 reduce.29
  284.1 3.2 reshape.831
  290.4 2.7 reshape.797
  297.9 14.4 %all_to_all.191 = f32[2,64,640]{2,0,1:T(2,128)S(1)} all-to-all(f32[2,64,640]{2,0,1:T(2,128)} %copy.340), channel_id=1, replica_groups=mesh['gx'=8,'gy'=4] {'gx'}, dimensions={1} | all-to-all | bytes 655360 | tf_op jit(solution)/shard_map/all_to_all | solution.py:95
  313.2 3.3 reshape.752
  316.5 4.3 copy.343
  320.8 5.2 %fusion.86 = f32[256,8,20,16,1]{0,2,4,3,1:T(8,128)S(1)} fusion(f32[16,8,2,20,16]{3,0,2,4,1:T(8,128)} %copy.343, f32[16,1,256]{2,0,1:T(8,128)S(1)} %copy-done.13, f32[16,1,256]{2,0,1:T(8,128)S(1)} %copy-done.16, f32[16]{0:T(128)S(1)} %copy-done.28), kind=kOutput, calls=%fused_computation.176 | convolution fusion | flops 251674624 | bytes 2981952 | tf_op jit(solution)/shard_map/kxpcy,kpz->cxyz/dot_general | solution.py:98
  326.0 10.5 %fusion.6 = f32[20,8,16,256]{3,0,2,1:T(8,128)S(1)} fusion(f32[256,8,20,16,1]{0,2,4,3,1:T(8,128)S(1)} %fusion.86, f32[20,8,16,256]{3,0,2,1:T(8,128)S(1)} %fusion.4, f32[20]{0:T(128)S(1)} %copy-done.31, f32[3,20,20]{2,1,0:T(8,128)} %param.6), kind=kOutput, calls=%fused_computation.10 | convolution fusion | flops 200540160 | bytes 7876688 | tf_op jit(solution)/shard_map/co,cxyz->oxyz/dot_general | solution.py:99
  338.2 10.5 %fusion.45 = f32[16,8,2,20,16]{3,0,4,1,2:T(8,128)} fusion(f32[20,8,16,256]{3,0,2,1:T(8,128)S(1)} %fusion.6, f32[256,16,1]{0,1,2:T(8,128)S(1)} %get-tuple-element.60, f32[256,16,1]{0,1,2:T(8,128)S(1)} %copy-done.12), kind=kOutput, calls=%fused_computation.88 | convolution fusion | flops 251666432 | bytes 2981888 | tf_op jit(solution)/shard_map/cxyz,zkp->kxpcy/dot_general | solution.py:79
  348.7 3.0 copy.345
  353.3 14.1 %all_to_all.192 = f32[16,8,640]{2,1,0:T(8,128)S(1)} all-to-all(f32[16,8,640]{2,1,0:T(8,128)} %reshape.753), channel_id=1, replica_groups=mesh['gx'=8,'gy'=4] {'gx'}, dimensions={0} | all-to-all | bytes 655360 | tf_op jit(solution)/shard_map/all_to_all | solution.py:82
  370.3 5.1 %fusion.56 = f32[2,20,16,128]{3,2,1,0:T(8,128)} fusion(f32[2,64,2,20,16]{4,3,2,1,0:T(8,128)S(1)} %reshape.754, f32[64,1,128]{2,0,1:T(8,128)S(1)} %copy.301, f32[64,1,128]{2,0,1:T(8,128)S(1)} %copy.300), kind=kOutput, calls=%fused_computation.102 | convolution fusion | flops 125845504 | bytes 720896 | tf_op jit(solution)/shard_map/kxpcy,xpm->kcym/dot_general | solution.py:84
  375.4 2.8 copy.348
  378.3 3.0 reshape.832
  381.2 3.7 all-to-all-start.9
  385.0 6.3 %squeeze.68 = f32[20,20,1024]{2,1,0:T(8,128)} reshape(f32[1,1,20,20,2,16,32]{6,5,4,3,2,1,0:T(8,128)} %get-tuple-element.28) | data formatting | bytes 3276800 | tf_op jit(solution)/shard_map/squeeze | solution.py:57
  391.3 6.3 %squeeze.70 = f32[20,20,1024]{2,1,0:T(8,128)} reshape(f32[1,1,20,20,2,16,32]{6,5,4,3,2,1,0:T(8,128)} %get-tuple-element.23) | data formatting | bytes 3276800 | tf_op jit(solution)/shard_map/squeeze | solution.py:57
  399.1 3.8 reshape.833
  402.9 3.8 copy.349
  410.0 2.2 multiply_reduce_fusion.3
  416.9 9.8 %all_to_all.193 = f32[4,1,20480]{2,1,0:T(1,128)S(1)} all-to-all(f32[4,1,20480]{2,1,0:T(1,128)S(1)} %reshape.834), channel_id=1, replica_groups=mesh['gx'=8,'gy'=4] {'gy'}, dimensions={0} | all-to-all | bytes 655360 | tf_op jit(solution)/shard_map/all_to_all | solution.py:91
  431.9 13.6 %all_to_all.194 = f32[2,64,640]{2,0,1:T(2,128)S(1)} all-to-all(f32[2,64,640]{2,0,1:T(2,128)S(1)} %copy.362), channel_id=1, replica_groups=mesh['gx'=8,'gy'=4] {'gx'}, dimensions={1} | all-to-all | bytes 655360 | tf_op jit(solution)/shard_map/all_to_all | solution.py:95
  446.8 3.2 copy.365
  450.1 5.3 %fusion.84 = f32[256,8,20,16,1]{0,2,4,3,1:T(8,128)S(1)} fusion(f32[16,8,2,20,16]{3,0,2,4,1:T(8,128)} %copy.365, f32[16,1,256]{2,0,1:T(8,128)S(1)} %copy-done.14, f32[16,1,256]{2,0,1:T(8,128)S(1)} %copy-done.17, f32[16]{0:T(128)S(1)} %copy-done.29), kind=kOutput, calls=%fused_computation.175 | convolution fusion | flops 251674624 | bytes 2981952 | tf_op jit(solution)/shard_map/kxpcy,kpz->cxyz/dot_general | solution.py:98
  455.4 10.4 %fusion.8 = f32[20,8,16,256]{3,0,2,1:T(8,128)S(1)} fusion(f32[256,8,20,16,1]{0,2,4,3,1:T(8,128)S(1)} %fusion.84, f32[20,8,16,256]{3,0,2,1:T(8,128)S(1)} %copy-done.4, f32[20]{0:T(128)S(1)} %copy-done.30, f32[3,20,20]{2,1,0:T(8,128)} %param.6), kind=kOutput, calls=%fused_computation.12 | convolution fusion | flops 200540160 | bytes 7876688 | tf_op jit(solution)/shard_map/co,cxyz->oxyz/dot_general | solution.py:99
  465.9 2.3 copy.367
  (180 shorter events, 85.0 us)
Async XLA Ops:
  0.1 0.6 copy-start.11
  17.9 37.2 %all-to-all-start = ((f32[16,8,640]{2,1,0:T(8,128)}), f32[16,8,640]{2,1,0:T(8,128)S(1)}, u32[]{:S(2)}, u32[]{:S(2)}) async-start(f32[16,8,640]{2,1,0:T(8,128)} %reshape.741), calls=%async_computation | async-start | bytes 655360 | tf_op jit(solution)/shard_map/all_to_all | solution.py:82
  60.8 8.6 %copy-start.25 = (f32[64,32,1]{0,1,2:T(8,128)S(1)}, f32[64,32,1]{0,1,2:T(8,128)}, u32[]{:S(2)}) copy-start(f32[64,32,1]{0,1,2:T(8,128)} %get-tuple-element.49) | copy-start | bytes 24580
  60.8 8.6 %copy-start.26 = (f32[64,32,1]{0,1,2:T(8,128)S(1)}, f32[64,32,1]{0,1,2:T(8,128)}, u32[]{:S(2)}) copy-start(f32[64,32,1]{0,1,2:T(8,128)} %get-tuple-element.50) | copy-start | bytes 24580
  60.8 8.6 %copy-start.27 = (f32[64,32,1]{0,1,2:T(8,128)S(1)}, f32[64,32,1]{0,1,2:T(8,128)}, u32[]{:S(2)}) copy-start(f32[64,32,1]{0,1,2:T(8,128)} %get-tuple-element.51) | copy-start | bytes 24580
  65.7 17.2 %all-to-all-start.1 = ((f32[4,1,20480]{2,1,0:T(1,128)}), f32[4,1,20480]{2,1,0:T(1,128)S(1)}, u32[]{:S(2)}, u32[]{:S(2)}) async-start(f32[4,1,20480]{2,1,0:T(1,128)} %reshape.824), calls=%async_computation.1 | async-start | bytes 655360 | tf_op jit(solution)/shard_map/all_to_all | solution.py:85
  69.5 24.8 %copy-start.5 = (f32[64,1,32,2]{0,2,1,3:T(8,128)}, f32[64,1,32,2]{0,2,1,3:T(8,128)S(1)}, u32[]{:S(2)}) copy-start(f32[64,1,32,2]{0,2,1,3:T(8,128)S(1)} %get-tuple-element.41) | copy-start | bytes 49156
  69.5 24.8 %copy-start.8 = (f32[64,1,32,2]{0,2,1,3:T(8,128)}, f32[64,1,32,2]{0,2,1,3:T(8,128)S(1)}, u32[]{:S(2)}) copy-start(f32[64,1,32,2]{0,2,1,3:T(8,128)S(1)} %get-tuple-element.42) | copy-start | bytes 49156
  75.8 6.4 %copy-start.22 = (f32[32,64,1]{1,0,2:T(8,128)S(1)}, f32[32,64,1]{1,0,2:T(8,128)}, u32[]{:S(2)}) copy-start(f32[32,64,1]{1,0,2:T(8,128)} %get-tuple-element.46) | copy-start | bytes 24580
  75.8 6.4 %copy-start.23 = (f32[32,64,1]{1,0,2:T(8,128)S(1)}, f32[32,64,1]{1,0,2:T(8,128)}, u32[]{:S(2)}) copy-start(f32[32,64,1]{1,0,2:T(8,128)} %get-tuple-element.47) | copy-start | bytes 24580
  75.8 6.4 %copy-start.24 = (f32[32,64,1]{1,0,2:T(8,128)S(1)}, f32[32,64,1]{1,0,2:T(8,128)}, u32[]{:S(2)}) copy-start(f32[32,64,1]{1,0,2:T(8,128)} %get-tuple-element.48) | copy-start | bytes 24580
  75.8 6.4 %copy-start.19 = (f32[64,64,1]{1,0,2:T(8,128)S(1)}, f32[64,64,1]{1,0,2:T(8,128)}, u32[]{:S(2)}) copy-start(f32[64,64,1]{1,0,2:T(8,128)} %get-tuple-element.53) | copy-start | bytes 49156
  75.8 6.4 %copy-start.20 = (f32[64,64,1]{1,0,2:T(8,128)S(1)}, f32[64,64,1]{1,0,2:T(8,128)}, u32[]{:S(2)}) copy-start(f32[64,64,1]{1,0,2:T(8,128)} %get-tuple-element.54) | copy-start | bytes 49156
  75.8 6.4 %copy-start.21 = (f32[64,64,1]{1,0,2:T(8,128)S(1)}, f32[64,64,1]{1,0,2:T(8,128)}, u32[]{:S(2)}) copy-start(f32[64,64,1]{1,0,2:T(8,128)} %get-tuple-element.57) | copy-start | bytes 49156
  94.2 1.6 copy-start.1
  99.6 7.3 %copy-start.18 = (f32[1,64,64,2]{2,1,3,0:T(8,128)S(1)}, f32[1,64,64,2]{2,1,3,0:T(8,128)}, u32[]{:S(2)}) copy-start(f32[1,64,64,2]{2,1,3,0:T(8,128)} %get-tuple-element.38) | copy-start | bytes 98308
  103.4 10.1 %all-to-all-start.2 = ((f32[4,1,20480]{2,1,0:T(1,128)}), f32[4,1,20480]{2,1,0:T(1,128)S(1)}, u32[]{:S(2)}, u32[]{:S(2)}) async-start(f32[4,1,20480]{2,1,0:T(1,128)} %reshape.826), calls=%async_computation.2 | async-start | bytes 655360 | tf_op jit(solution)/shard_map/all_to_all | solution.py:91
  118.1 11.5 %copy-start = (f32[20,8,16,256]{3,2,1,0:T(8,128)S(1)}, f32[20,8,16,256]{3,2,1,0:T(8,128)}, u32[]{:S(2)}) copy-start(f32[20,8,16,256]{3,2,1,0:T(8,128)} %param.4) | copy-start | bytes 7864324
  122.0 16.2 %all-to-all-start.3 = ((f32[2,64,640]{2,0,1:T(2,128)}), f32[2,64,640]{2,0,1:T(2,128)S(1)}, u32[]{:S(2)}, u32[]{:S(2)}) async-start(f32[2,64,640]{2,0,1:T(2,128)} %copy.317), calls=%async_computation.3 | async-start | bytes 655360 | tf_op jit(solution)/shard_map/all_to_all | solution.py:95
  141.1 3.1 copy-start.13
  141.1 3.1 copy-start.15
  151.2 7.0 %copy-start.12 = (f32[256,16,1]{0,1,2:T(8,128)S(1)}, f32[256,16,1]{0,1,2:T(8,128)}, u32[]{:S(2)}) copy-start(f32[256,16,1]{0,1,2:T(8,128)} %copy-done.11) | copy-start | bytes 49156
  209.7 16.8 %all-to-all-start.5 = ((f32[4,1,20480]{2,1,0:T(1,128)}), f32[4,1,20480]{2,1,0:T(1,128)}, u32[]{:S(2)}, u32[]{:S(2)}) async-start(f32[4,1,20480]{2,1,0:T(1,128)} %reshape.828), calls=%async_computation.5 | async-start | bytes 655360 | tf_op jit(solution)/shard_map/all_to_all | solution.py:85
  234.4 8.6 %copy-start.6 = (f32[64,1,32,2]{0,2,1,3:T(8,128)S(1)}, f32[64,1,32,2]{0,2,1,3:T(8,128)}, u32[]{:S(2)}) copy-start(f32[64,1,32,2]{0,2,1,3:T(8,128)} %copy-done.5) | copy-start | bytes 49156
  234.4 8.6 %copy-start.9 = (f32[64,1,32,2]{0,2,1,3:T(8,128)S(1)}, f32[64,1,32,2]{0,2,1,3:T(8,128)}, u32[]{:S(2)}) copy-start(f32[64,1,32,2]{0,2,1,3:T(8,128)} %copy-done.8) | copy-start | bytes 49156
  316.5 4.3 copy-start.16
  316.5 4.3 copy-start.28
  320.8 5.2 %copy-start.31 = (f32[20]{0:T(128)S(1)}, f32[20]{0:T(128)}, u32[]{:S(2)}) copy-start(f32[20]{0:T(128)} %get-tuple-element.45) | copy-start | bytes 244
  336.5 1.6 copy-start.3
  381.2 16.3 %all-to-all-start.9 = ((f32[4,1,20480]{2,1,0:T(1,128)}), f32[4,1,20480]{2,1,0:T(1,128)S(1)}, u32[]{:S(2)}, u32[]{:S(2)}) async-start(f32[4,1,20480]{2,1,0:T(1,128)} %reshape.832), calls=%async_computation.9 | async-start | bytes 655360 | tf_op jit(solution)/shard_map/all_to_all | solution.py:85
  402.9 5.5 %copy-start.7 = (f32[64,1,32,2]{0,2,1,3:T(8,128)S(1)}, f32[64,1,32,2]{0,2,1,3:T(8,128)}, u32[]{:S(2)}) copy-start(f32[64,1,32,2]{0,2,1,3:T(8,128)} %copy-done.5) | copy-start | bytes 49156
  402.9 5.5 %copy-start.10 = (f32[64,1,32,2]{0,2,1,3:T(8,128)S(1)}, f32[64,1,32,2]{0,2,1,3:T(8,128)}, u32[]{:S(2)}) copy-start(f32[64,1,32,2]{0,2,1,3:T(8,128)} %copy-done.8) | copy-start | bytes 49156
  408.4 1.6 copy-start.2
  446.8 3.3 copy-start.14
  446.8 3.3 copy-start.17
  446.8 3.3 copy-start.29
  450.1 5.3 %copy-start.4 = (f32[20,8,16,256]{3,0,2,1:T(8,128)S(1)}, f32[20,8,16,256]{3,0,2,1:T(8,128)}, u32[]{:S(2)}) copy-start(f32[20,8,16,256]{3,0,2,1:T(8,128)} %copy-done.3) | copy-start | bytes 7864324
  450.1 5.3 %copy-start.30 = (f32[20]{0:T(128)S(1)}, f32[20]{0:T(128)}, u32[]{:S(2)}) copy-start(f32[20]{0:T(128)} %get-tuple-element.43) | copy-start | bytes 244
where the time goes:
time: 477 us; the launch traced here: 468 us
  local copies, waits for them, and re-layouts  214 us (45%)
  matrix products  106 us (22%)
  blocking collectives  77.7 us (16%)
  other arithmetic  33 us (7%)
  starting transfers between devices  28.9 us (6%)
  waiting for transfers between devices  7.53 us (2%)
    squeeze x12, local copies, waits for them, and re-layouts, mix_modes(): real_part = paired(flat[0], kernel[0]) - paired(flat[1], kernel[1])  41.4 us
    unnamed x76, local copies, waits for them, and re-layouts  36.9 us
    dot_general x3, matrix products, shards(): jnp.einsum('cxyz,zkp->kxpcy', current, table_z, precision=highest)  33.6 us
    slice x10, local copies, waits for them, and re-layouts, mix_modes(): real_part = paired(flat[0], kernel[0]) - paired(flat[1], kernel[1])  30.4 us
    all_to_all x2, blocking collectives, shards(): lax.all_to_all(spectrum, 'gx', split_axis=0, concat_axis=1, tiled=True)  28.6 us
    all_to_all x2, blocking collectives, shards(): lax.all_to_all(planes, 'gx', split_axis=1, concat_axis=0, tiled=True)  28 us
    dot_general x3, matrix products, shards(): jnp.einsum('co,cxyz->oxyz', point_weight[layer_index], current, precision...  27.3 us
    all_to_all x2, blocking collectives, shards(): lines = lax.all_to_all(lines, 'gy', split_axis=2, concat_axis=3, tiled=True)  21 us
  transfers between devices with their start and end apart: 6, of which 2 were waited for; matrix products, arithmetic and copies ran while one was open for 16% of the time, Pallas kernels for 0%

commit v1 on v0

v1 whole, which is shorter than its diff:
```python
import functools

import jax
import jax.numpy as jnp
import numpy as np
from jax import lax
from jax.experimental import pallas as pl
from jax.experimental.pallas import tpu as pltpu
from jax.sharding import PartitionSpec as P

MZ = 16
MX = 64
MY = 32
LANES = 128
OCT = 8


def mode_list(count, points):
    half = count // 2
    lower = np.arange(half)
    return np.concatenate([lower, points - half + lower])


def wave_tables(modes, points):
    phase = 2.0 * np.pi / points * ((modes[:, None] * np.arange(points)[None, :]) % points)
    return np.cos(phase), np.sin(phase)


def split(value):
    high = value.astype(jnp.bfloat16)
    low = (value - high.astype(jnp.float32)).astype(jnp.bfloat16)
    return high, low


def outer_split(value):
    high = lax.reduce_precision(value, 8, 7)
    return high.astype(jnp.bfloat16), (value - high).astype(jnp.bfloat16)


def dot3(left, right):
    def one(a, b):
        return jnp.dot(a, b, preferred_element_type=jnp.float32)

    return one(left[0], right[0]) + one(left[1], right[0]) + one(left[0], right[1])


def time_kernel(has_inverse, has_forward, *refs):
    refs = list(refs)
    u_ref = refs.pop(0)
    if has_inverse:
        planes_ref, inv_hi, inv_lo, mix_hi, mix_lo, bias_ref = (refs.pop(0) for _ in range(6))
    if has_forward:
        fwd_hi, fwd_lo = refs.pop(0), refs.pop(0)
    if has_inverse:
        out_ref = refs.pop(0)
    if has_forward:
        spec_ref = refs.pop(0)
    if has_inverse:
        p_hi, p_lo = refs.pop(0), refs.pop(0)
    if has_forward:
        acc = refs.pop(0)
    step = pl.program_id(0)
    channels, _, rows_y, depth = u_ref.shape
    cg = LANES // (2 * rows_y)
    groups = channels // cg

    if has_inverse:

        @pl.when(step == 0)
        def _():
            modes, rows_x, width = planes_ref.shape
            flat = planes_ref[...].reshape(modes * rows_x, width)
            for g in range(groups):
                turned = flat[:, g * LANES : (g + 1) * LANES].T
                high, low = split(turned)
                for c in range(cg):
                    for q in range(2):
                        src = slice((c * 2 + q) * rows_y, (c * 2 + q + 1) * rows_y)
                        dst = slice((g * cg + c) * rows_y, (g * cg + c + 1) * rows_y)
                        n = modes * rows_x
                        p_hi[dst, q * n : (q + 1) * n] = high[src]
                        p_lo[dst, q * n : (q + 1) * n] = low[src]

        wave = dot3((p_hi[...], p_lo[...]), (inv_hi[0], inv_lo[0]))
        wave = wave.reshape(channels, rows_y, depth)
        mixer = (mix_hi[0], mix_lo[0])
        for part in range(rows_y // OCT):
            rows = slice(part * OCT, (part + 1) * OCT)
            x = u_ref[:, 0, rows, :].reshape(channels * OCT, depth)
            local = dot3(mixer, split(x))
            v = wave[:, rows, :].reshape(channels * OCT, depth) + local + bias_ref[0]
            v = v * (lax.erf(v * np.float32(np.sqrt(0.5))) + 1.0) * 0.5
            out_ref[:, 0, rows, :] = v.reshape(channels, OCT, depth)

    if has_forward:
        source = out_ref if has_inverse else u_ref
        g_split = split(source[:, 0, :, :].reshape(channels * rows_y, depth))
        term = dot3(g_split, (fwd_hi[0], fwd_lo[0]))

        @pl.when(step == 0)
        def _():
            acc[...] = term

        @pl.when(step > 0)
        def _():
            acc[...] += term

        @pl.when(step == pl.num_programs(0) - 1)
        def _():
            modes, rows_x, width = spec_ref.shape
            n = modes * rows_x
            for g in range(groups):
                pieces = []
                for c in range(cg):
                    for q in range(2):
                        rows = slice((g * cg + c) * rows_y, (g * cg + c + 1) * rows_y)
                        pieces.append(acc[rows, q * n : (q + 1) * n])
                turned = jnp.concatenate(pieces, axis=0).T
                spec_ref[:, :, g * LANES : (g + 1) * LANES] = turned.reshape(modes, rows_x, LANES)


def time_step(layer, u, planes, tables):
    channels, rows_x, rows_y, depth = u.shape
    has_inverse = planes is not None
    has_forward = tables["fwd"] is not None
    width = channels * 2 * rows_y
    n = MZ * rows_x
    block = pl.BlockSpec((channels, 1, rows_y, depth), lambda s: (0, s, 0, 0))
    args, specs = [u], [block]
    if has_inverse:
        args += [planes, *tables["inv"], *tables["mix"], tables["bias"]]
        specs += [pl.BlockSpec((MZ, rows_x, width), lambda s: (0, 0, 0))]
        specs += [pl.BlockSpec((1, 2 * n, depth), lambda s: (s, 0, 0))] * 2
        side = channels * OCT
        specs += [pl.BlockSpec((1, side, side), lambda s: (layer, 0, 0))] * 2
        specs += [pl.BlockSpec((1, side, depth), lambda s: (layer, 0, 0))]
    if has_forward:
        args += [*tables["fwd"]]
        specs += [pl.BlockSpec((1, depth, 2 * n), lambda s: (s, 0, 0))] * 2
    outs, out_specs, scratch = [], [], []
    if has_inverse:
        outs.append(jax.ShapeDtypeStruct(u.shape, jnp.float32))
        out_specs.append(block)
        scratch += [pltpu.VMEM((channels * rows_y, 2 * n), jnp.bfloat16)] * 2
    if has_forward:
        outs.append(jax.ShapeDtypeStruct((MZ, rows_x, width), jnp.float32))
        out_specs.append(pl.BlockSpec((MZ, rows_x, width), lambda s: (0, 0, 0)))
        scratch += [pltpu.VMEM((channels * rows_y, 2 * n), jnp.float32)]
    return pl.pallas_call(
        functools.partial(time_kernel, has_inverse, has_forward),
        grid=(rows_x,),
        in_specs=specs,
        out_specs=out_specs,
        out_shape=outs,
        scratch_shapes=scratch,
        name="time_step",
    )(*args)


def x_kernel(sign, rows_y, data_ref, t_hi, t_lo, out_ref):
    src, modes_z, per_src, width = data_ref.shape
    dst, _, per_dst, _ = out_ref.shape
    n = dst * per_dst
    lane = lax.broadcasted_iota(jnp.int32, (n, LANES), 1)
    real_lane = (lane // rows_y) % 2 == 0
    for k in range(modes_z):
        d = split(data_ref[:, k].reshape(src * per_src, width))
        both = dot3((t_hi[...], t_lo[...]), d)
        for g in range(width // LANES):
            cols = slice(g * LANES, (g + 1) * LANES)
            cosine, sine = both[:n, cols], both[n:, cols]
            ahead = pltpu.roll(sine, LANES - rows_y, axis=1)
            behind = pltpu.roll(sine, rows_y, axis=1)
            swapped = jnp.where(real_lane, ahead, -behind)
            value = cosine + swapped if sign > 0 else cosine - swapped
            out_ref[:, k, :, cols] = value.reshape(dst, per_dst, LANES)


def x_step(sign, rows_y, data, table, dst):
    src, modes_z, per_src, width = data.shape
    per_dst = table[0].shape[0] // 2 // dst
    return pl.pallas_call(
        functools.partial(x_kernel, sign, rows_y),
        out_shape=jax.ShapeDtypeStruct((dst, modes_z, per_dst, width), jnp.float32),
        name="x_step",
    )(data, *table)


def y_kernel(rows_y, data_ref, w_ref, f_hi, f_lo, i_hi, i_lo, out_ref, left_ref, s_ref, m_ref):
    step = pl.program_id(0)
    count_y, modes_z, local_x, width = data_ref.shape
    groups = width // LANES
    cg = LANES // (2 * rows_y)
    rows = modes_z * local_x
    _, _, channels, per_step, _, _, modes_y = w_ref.shape

    @pl.when(step == 0)
    def _():
        for y in range(count_y):
            block = data_ref[y].reshape(rows, width)
            for g in range(groups):
                left_ref[g * rows : (g + 1) * rows, y * LANES : (y + 1) * LANES] = block[
                    :, g * LANES : (g + 1) * LANES
                ]
        full = dot3(split(left_ref[...]), (f_hi[...], f_lo[...]))
        for g in range(groups):
            for c in range(cg):
                for q in range(2):
                    start = (c * 2 + q) * modes_y
                    s_ref[g * cg + c, q] = full[
                        g * rows : (g + 1) * rows, start : start + modes_y
                    ]

    for o in range(per_step):
        real = jnp.zeros((rows, modes_y), jnp.float32)
        imag = jnp.zeros((rows, modes_y), jnp.float32)
        for c in range(channels):
            wr = w_ref[0, 0, c, o].reshape(rows, modes_y)
            wi = w_ref[0, 1, c, o].reshape(rows, modes_y)
            sr, si = s_ref[c, 0], s_ref[c, 1]
            real += wr * sr - wi * si
            imag += wr * si + wi * sr
        m_ref[step * per_step + o, 0] = real
        m_ref[step * per_step + o, 1] = imag

    @pl.when(step == pl.num_programs(0) - 1)
    def _():
        blocks = []
        for g in range(groups):
            pieces = [m_ref[g * cg + c, q] for c in range(cg) for q in range(2)]
            blocks.append(jnp.concatenate(pieces, axis=1))
        lines = dot3(split(jnp.concatenate(blocks, axis=0)), (i_hi[...], i_lo[...]))
        for y in range(count_y):
            for g in range(groups):
                piece = lines[g * rows : (g + 1) * rows, y * LANES : (y + 1) * LANES]
                out_ref[y, :, :, g * LANES : (g + 1) * LANES] = piece.reshape(
                    modes_z, local_x, LANES
                )


def y_step(layer, rows_y, data, weights, forward, inverse):
    count_y, modes_z, local_x, width = data.shape
    _, _, channels, _, _, _, modes_y = weights.shape
    per_step = 4 if channels % 4 == 0 else 1
    rows = modes_z * local_x
    groups = width // LANES
    cg = LANES // (2 * rows_y)
    whole = lambda s: (0, 0)
    return pl.pallas_call(
        functools.partial(y_kernel, rows_y),
        grid=(channels // per_step,),
        in_specs=[
            pl.BlockSpec(data.shape, lambda s: (0, 0, 0, 0)),
            pl.BlockSpec(
                (1, 2, channels, per_step, modes_z, local_x, modes_y),
                lambda s: (layer, 0, 0, s, 0, 0, 0),
            ),
            pl.BlockSpec(forward[0].shape, whole),
            pl.BlockSpec(forward[1].shape, whole),
            pl.BlockSpec(inverse[0].shape, whole),
            pl.BlockSpec(inverse[1].shape, whole),
        ],
        out_specs=pl.BlockSpec(data.shape, lambda s: (0, 0, 0, 0)),
        out_shape=jax.ShapeDtypeStruct(data.shape, jnp.float32),
        scratch_shapes=[
            pltpu.VMEM((groups * rows, count_y * LANES), jnp.float32),
            pltpu.VMEM((channels, 2, rows, modes_y), jnp.float32),
            pltpu.VMEM((channels, 2, rows, modes_y), jnp.float32),
        ],
        name="y_step",
    )(data, weights, *forward, *inverse)


def time_table(rows_x, depth, total):
    cosine, sine = wave_tables(np.arange(MZ), depth)
    weight = np.where(np.arange(MZ) == 0, 1.0, 2.0)[:, None] / total
    fwd = jnp.asarray(np.stack([cosine, -sine]), jnp.float32)
    inv = jnp.asarray(np.stack([cosine * weight, -sine * weight]), jnp.float32)
    n = 2 * MZ * rows_x
    row = lax.broadcasted_iota(jnp.int32, (rows_x, n, depth), 0)
    col = lax.broadcasted_iota(jnp.int32, (rows_x, n, depth), 1) % rows_x
    wide = jnp.repeat(inv.reshape(2 * MZ, depth), rows_x, axis=0)[None]
    inverse = jnp.where(row == col, wide, 0.0)
    row = lax.broadcasted_iota(jnp.int32, (rows_x, depth, n), 0)
    col = lax.broadcasted_iota(jnp.int32, (rows_x, depth, n), 2) % rows_x
    wide = jnp.repeat(fwd.reshape(2 * MZ, depth).T, rows_x, axis=1)[None]
    forward = jnp.where(row == col, wide, 0.0)
    return outer_split(forward), outer_split(inverse)


def constant_split(table):
    high = np.asarray(table, np.float32).astype(jnp.bfloat16)
    low = (np.asarray(table, np.float32) - high.astype(np.float32)).astype(jnp.bfloat16)
    return jnp.asarray(high), jnp.asarray(low)


def y_tables(points_y, rows_y):
    cosine, sine = wave_tables(mode_list(MY, points_y), points_y)
    count = points_y // rows_y
    cg = LANES // (2 * rows_y)
    cosine = cosine.reshape(MY, count, rows_y)
    sine = sine.reshape(MY, count, rows_y)
    fwd = np.stack([np.stack([cosine, -sine]), np.stack([sine, cosine])])
    inv = np.stack([np.stack([cosine, sine]), np.stack([-sine, cosine])])
    eye = np.eye(cg)
    fwd = np.einsum("ab,rqmgy->garybqm", eye, fwd).reshape(count * LANES, cg * 2 * MY)
    inv = np.einsum("ab,qrmgy->aqmgbry", eye, inv).reshape(cg * 2 * MY, count * LANES)
    return constant_split(fwd), constant_split(inv)


def shards(field, spectral_weight, point_weight, bias):
    channels, rows_x, rows_y, depth = field.shape
    layers = spectral_weight.shape[0]
    count_x = lax.axis_size("gx")
    count_y = lax.axis_size("gy")
    points_x = rows_x * count_x
    points_y = rows_y * count_y
    local_z = MZ // count_x
    local_x = MX // count_y
    fwd_z, inv_z = time_table(rows_x, depth, float(points_x * points_y * depth))
    cosine, sine = wave_tables(mode_list(MX, points_x), points_x)
    fwd_x = constant_split(np.concatenate([cosine, sine], 0))
    inv_x = constant_split(np.concatenate([cosine.T, sine.T], 0))
    fwd_y, inv_y = y_tables(points_y, rows_y)
    eye = jnp.eye(OCT, dtype=jnp.float32)
    mixer = jnp.einsum("lco,yv->loycv", point_weight, eye, precision=lax.Precision.HIGHEST)
    mixer = outer_split(mixer.reshape(layers, channels * OCT, channels * OCT))
    wide_bias = jnp.broadcast_to(
        jnp.repeat(bias, OCT, axis=1)[:, :, None], (layers, channels * OCT, depth)
    )
    tables = {"fwd": fwd_z, "inv": inv_z, "mix": mixer, "bias": wide_bias}
    last = dict(tables, fwd=None)

    current = field
    (spectrum,) = time_step(0, current, None, tables)
    for layer in range(layers):
        data = spectrum.reshape(count_x, local_z, rows_x, -1)
        data = lax.all_to_all(data, "gx", 0, 0)
        data = x_step(1, rows_y, data, fwd_x, count_y)
        data = lax.all_to_all(data, "gy", 0, 0)
        data = y_step(layer, rows_y, data, spectral_weight, fwd_y, inv_y)
        data = lax.all_to_all(data, "gy", 0, 0)
        data = x_step(-1, rows_y, data, inv_x, count_x)
        data = lax.all_to_all(data, "gx", 0, 0)
        planes = data.reshape(MZ, rows_x, -1)
        if layer + 1 < layers:
            current, spectrum = time_step(layer, current, planes, tables)
        else:
            (current,) = time_step(layer, current, planes, last)
    return current


def solution(mesh):
    return jax.shard_map(
        shards,
        mesh=mesh,
        in_specs=(P(None, "gx", "gy", None), P(None, None, None, None, "gx", "gy", None), P(), P()),
        out_specs=P(None, "gx", "gy", None),
        check_vma=False,
    )
```

time: 477 us -> 241 us (0.51); the launches traced: 468 us -> 239 us
  local copies, waits for them, and re-layouts: 214 us -> 7.72 us
  matrix products: 106 us -> 0 us
  Pallas kernels: 0 us -> 77.8 us
  blocking collectives: 77.7 us -> 131 us
  other arithmetic: 33 us -> 6.65 us
  starting transfers between devices: 28.9 us -> 6.89 us
    dot_general x21 -> x0, matrix products: 106 us -> none  [the longest x3 33.6 us: shards(): jnp.einsum('cxyz,zkp->kxpcy', current, table_z, precision=highest)]
    pallas_call x0 -> x13, Pallas kernels: none -> 77.8 us  [the longest x4 35.5 us: time_step(): pl.pallas_call(functools.partial(time_kernel, has_inverse, has_forward),...]
    all_to_all x6 -> x10, blocking collectives: 77.7 us -> 131 us  [the longest x5 77 us: shards(): data = lax.all_to_all(data, 'gx', 0, 0)]
    reshape x21 -> x1, local copies, waits for them, and re-layouts: 46 us -> 4.11 us  [shards(): mixer = outer_split(mixer.reshape(layers, channels * OCT, channels * OCT))]
    squeeze x12 -> x0, local copies, waits for them, and re-layouts: 41.4 us -> none  [mix_modes(): real_part = paired(flat[0], kernel[0]) - paired(flat[1], kernel[1])]
    unnamed x76 -> x9, local copies, waits for them, and re-layouts: 36.9 us -> 0.84 us
    slice x10 -> x0, local copies, waits for them, and re-layouts: 30.4 us -> none  [mix_modes(): real_part = paired(flat[0], kernel[0]) - paired(flat[1], kernel[1])]
    all_to_all x22 -> x0, local copies, waits for them, and re-layouts: 27.1 us -> none  [the longest x4 12.9 us: shards(): lax.all_to_all(spectrum, 'gy', split_axis=3, concat_axis=2, tiled=True)]
  transfers between devices with their start and end apart: 6 -> 2, of which waited for: 2 -> 2; matrix products, arithmetic and copies ran while one was open for 16% -> 3% of each run, Pallas kernels for 0% -> 0%
where the time goes in v1:
time: 241 us; the launch traced here: 239 us
  blocking collectives  131 us (54%)
  Pallas kernels  77.8 us (32%)
  waiting for transfers between devices  8.6 us (4%)
  local copies, waits for them, and re-layouts  7.72 us (3%)
  starting transfers between devices  6.89 us (3%)
  other arithmetic  6.65 us (3%)
    all_to_all x5, blocking collectives, shards(): data = lax.all_to_all(data, 'gx', 0, 0)  77 us
    all_to_all x5, blocking collectives, shards(): data = lax.all_to_all(data, 'gy', 0, 0)  54.3 us
    pallas_call x4, Pallas kernels, time_step(): pl.pallas_call(functools.partial(time_kernel, has_inverse, has_forward),...  35.5 us
    pallas_call x3, Pallas kernels, y_step(): pl.pallas_call(functools.partial(y_kernel, rows_y), grid=(channels // per...  28.8 us
    pallas_call x6, Pallas kernels, x_step(): pl.pallas_call(functools.partial(x_kernel, sign, rows_y), out_shape=jax.S...  13.4 us
    all_to_all x1, waiting for transfers between devices, shards(): data = lax.all_to_all(data, 'gy', 0, 0)  6.55 us
  transfers between devices with their start and end apart: 2, of which 2 were waited for; matrix products, arithmetic and copies ran while one was open for 3% of the time, Pallas kernels for 0%

profile of v1, /device:TPU:0, one launch (start us, length us, event | category | flops | bytes accessed | tf_op | source)
XLA Modules:
  0.0 239.0 jit_solution(7842971171336700649)
XLA Ops:
  0.0 0.8 broadcast_bitcast_fusion.1
  0.8 0.1 copy.16
  0.9 0.8 broadcast_bitcast_fusion
  1.7 2.8 %fusion.1 = (bf16[8,256,256]{2,1,0:T(8,128)(2,1)}, bf16[8,256,256]{2,1,0:T(8,128)(2,1)}, bf16[8,256,256]{2,1,0:T(8,128)(2,1)}, bf16[8,256,256]{2,1,0:T(8,128)(2,1)}) fusion(f32[256,256]{1,0:T(8,128)S(1)} %broadcast_bitcast_fusion, s32[256]{0:T(256)S(1)} %get-tuple-element.21, s32[256]{0:T(256)S(1)} %get-tuple-element.22, ...), kind=kLoop, calls=%fused_computation.6 | loop fusion | flops 7340032 | bytes 4720896 | tf_op jit(solution)/shard_map/convert_element_type | solution.py:37
  4.5 6.9 %time_step.4 = f32[16,8,640]{2,1,0:T(8,128)} custom-call(f32[20,8,16,256]{3,2,1,0:T(8,128)} %refs_0_.3, bf16[8,256,256]{2,1,0:T(8,128)(2,1)} %get-tuple-element.19.refs_1_.refs_7_, bf16[8,256,256]{2,1,0:T(8,128)(2,1)} %get-tuple-element.20.refs_2_.refs_8_), custom_call_target="tpu_custom_call" | custom-call | tf_op jit(solution)/shard_map/time_step/pallas_call | solution.py:149
  11.4 18.3 %all_to_all.60.data_ref = f32[8,2,8,640]{3,2,1,0:T(8,128)} all-to-all(f32[8,2,8,640]{3,2,1,0:T(8,128)} %bitcast.15), channel_id=1, replica_groups=mesh['gx'=8,'gy'=4] {'gx'}, dimensions={0} | all-to-all | bytes 655360 | tf_op jit(solution)/shard_map/all_to_all | solution.py:338
  29.7 2.2 x_step.6
  32.0 10.9 %all_to_all.61.data_ref = f32[4,2,16,640]{3,2,1,0:T(8,128)} all-to-all(f32[4,2,16,640]{3,2,1,0:T(8,128)} %x_step.6), channel_id=1, replica_groups=mesh['gx'=8,'gy'=4] {'gy'}, dimensions={0} | all-to-all | bytes 655360 | tf_op jit(solution)/shard_map/all_to_all | solution.py:340
  42.8 0.0 copy-start.2
  42.8 9.6 %y_step.3 = f32[4,2,16,640]{3,2,1,0:T(8,128)} custom-call(f32[4,2,16,640]{3,2,1,0:T(8,128)} %all_to_all.61.data_ref, f32[3,2,20,20,2,16,32]{6,5,4,3,2,1,0:T(8,128)} %w_ref.5, bf16[512,256]{1,0:T(8,128)(2,1)} %constant.41.clone.f_hi, bf16[512,256]{1,0:T(8,128)(2,1)} %constant.42.clone.f_lo, bf16[256,512]{1,0:T(8,128)(2,1)} %constant.43.clone.i_hi, ...), custom_call_target="tpu_custom_call" | custom-call | tf_op jit(solution)/shard_map/y_step/pallas_call | solution.py:249
  52.5 3.5 %all-to-all-start.2 = ((f32[4,2,16,640]{3,2,1,0:T(8,128)}), f32[4,2,16,640]{3,2,1,0:T(8,128)S(1)}, u32[]{:S(2)}, u32[]{:S(2)}) async-start(f32[4,2,16,640]{3,2,1,0:T(8,128)} %y_step.3), calls=%async_computation.2 | async-start | bytes 655360 | tf_op jit(solution)/shard_map/all_to_all | solution.py:342
  55.9 0.0 copy-done.2
  55.9 0.1 copy.17
  56.0 6.6 %all-to-all-done.2.data_ref = f32[4,2,16,640]{3,2,1,0:T(8,128)S(1)} async-done(((f32[4,2,16,640]{3,2,1,0:T(8,128)}), f32[4,2,16,640]{3,2,1,0:T(8,128)S(1)}, u32[]{:S(2)}, u32[]{:S(2)}) %all-to-all-start.2) | async-done | bytes 327712 | tf_op jit(solution)/shard_map/all_to_all | solution.py:342
  62.6 0.0 copy-start.1
  62.6 0.7 copy-done.1
  63.3 2.2 x_step.7
  65.6 3.4 %all-to-all-start.3 = ((f32[8,2,8,640]{3,2,1,0:T(8,128)}), f32[8,2,8,640]{3,2,1,0:T(8,128)S(1)}, u32[]{:S(2)}, u32[]{:S(2)}) async-start(f32[8,2,8,640]{3,2,1,0:T(8,128)} %x_step.7), calls=%async_computation.3 | async-start | bytes 655360 | tf_op jit(solution)/shard_map/all_to_all | solution.py:344
  69.0 3.0 %multiply_bitcast_fusion = f32[3,20,8,20,8]{4,3,2,1,0:T(8,128)} fusion(f32[3,20,20]{1,2,0:T(8,128)S(1)} %copy.17, f32[8,8]{1,0:T(8,128)S(1)} %fusion.3), kind=kLoop, calls=%fused_computation | loop fusion | flops 76800 | bytes 312256 | tf_op jit(solution)/shard_map/lco,yv->loycv/transpose | solution.py:326
  72.0 0.0 copy-start.3
  72.0 4.1 %reshape.34 = f32[3,160,160]{2,1,0:T(8,128)S(1)} reshape(f32[3,20,8,20,8]{4,3,2,1,0:T(8,128)} %multiply_bitcast_fusion) | data formatting | bytes 614400 | tf_op jit(solution)/shard_map/reshape | solution.py:327
  76.1 0.0 copy-done.3
  76.1 0.1 broadcast_in_dim.45
  76.2 0.1 broadcast_in_dim.46
  76.3 0.9 fusion.2
  77.2 2.0 all-to-all-done.3
  79.2 0.0 copy-start
  79.2 0.9 broadcast_in_dim.47.refs_6_
  80.1 0.0 copy-done
  80.1 10.2 %time_step.5 = (f32[20,8,16,256]{3,2,1,0:T(8,128)}, f32[16,8,640]{2,1,0:T(8,128)}) custom-call(f32[20,8,16,256]{3,2,1,0:T(8,128)} %refs_0_.3, f32[16,8,640]{2,1,0:T(8,128)} %bitcast.12, bf16[8,256,256]{2,1,0:T(8,128)(2,1)} %get-tuple-element.16.refs_2_, bf16[8,256,256]{2,1,0:T(8,128)(2,1)} %get-tuple-element.15.refs_3_, ...), custom_call_target="tpu_custom_call" | custom-call | tf_op jit(solution)/shard_map/time_step/pallas_call | solution.py:149
  90.3 14.4 %all_to_all.62.data_ref = f32[8,2,8,640]{3,2,1,0:T(8,128)} all-to-all(f32[8,2,8,640]{3,2,1,0:T(8,128)} %bitcast.17), channel_id=1, replica_groups=mesh['gx'=8,'gy'=4] {'gx'}, dimensions={0} | all-to-all | bytes 655360 | tf_op jit(solution)/shard_map/all_to_all | solution.py:338
  104.7 2.2 x_step.8
  107.0 10.9 %all_to_all.63.data_ref = f32[4,2,16,640]{3,2,1,0:T(8,128)} all-to-all(f32[4,2,16,640]{3,2,1,0:T(8,128)} %x_step.8), channel_id=1, replica_groups=mesh['gx'=8,'gy'=4] {'gy'}, dimensions={0} | all-to-all | bytes 655360 | tf_op jit(solution)/shard_map/all_to_all | solution.py:340
  117.8 9.6 %y_step.4 = f32[4,2,16,640]{3,2,1,0:T(8,128)} custom-call(f32[4,2,16,640]{3,2,1,0:T(8,128)} %all_to_all.63.data_ref, f32[3,2,20,20,2,16,32]{6,5,4,3,2,1,0:T(8,128)} %w_ref.5, bf16[512,256]{1,0:T(8,128)(2,1)} %constant.41.clone.f_hi, bf16[512,256]{1,0:T(8,128)(2,1)} %constant.42.clone.f_lo, bf16[256,512]{1,0:T(8,128)(2,1)} %constant.43.clone.i_hi, ...), custom_call_target="tpu_custom_call" | custom-call | tf_op jit(solution)/shard_map/y_step/pallas_call | solution.py:249
  127.4 10.9 %all_to_all.64.data_ref = f32[4,2,16,640]{3,2,1,0:T(8,128)} all-to-all(f32[4,2,16,640]{3,2,1,0:T(8,128)} %y_step.4), channel_id=1, replica_groups=mesh['gx'=8,'gy'=4] {'gy'}, dimensions={0} | all-to-all | bytes 655360 | tf_op jit(solution)/shard_map/all_to_all | solution.py:342
  138.3 2.2 x_step.9
  140.5 15.2 %all_to_all.65 = f32[8,2,8,640]{3,2,1,0:T(8,128)} all-to-all(f32[8,2,8,640]{3,2,1,0:T(8,128)} %x_step.9), channel_id=1, replica_groups=mesh['gx'=8,'gy'=4] {'gx'}, dimensions={0} | all-to-all | bytes 655360 | tf_op jit(solution)/shard_map/all_to_all | solution.py:344
  155.7 10.2 %time_step.6 = (f32[20,8,16,256]{3,2,1,0:T(8,128)}, f32[16,8,640]{2,1,0:T(8,128)}) custom-call(f32[20,8,16,256]{3,2,1,0:T(8,128)} %get-tuple-element.9.refs_0_, f32[16,8,640]{2,1,0:T(8,128)} %bitcast.14, bf16[8,256,256]{2,1,0:T(8,128)(2,1)} %get-tuple-element.16.refs_2_, bf16[8,256,256]{2,1,0:T(8,128)(2,1)} %get-tuple-element.15.refs_3_, ...), custom_call_target="tpu_custom_call" | custom-call | tf_op jit(solution)/shard_map/time_step/pallas_call | solution.py:149
  165.9 13.9 %all_to_all.66.data_ref = f32[8,2,8,640]{3,2,1,0:T(8,128)} all-to-all(f32[8,2,8,640]{3,2,1,0:T(8,128)} %bitcast.16), channel_id=1, replica_groups=mesh['gx'=8,'gy'=4] {'gx'}, dimensions={0} | all-to-all | bytes 655360 | tf_op jit(solution)/shard_map/all_to_all | solution.py:338
  179.8 2.2 x_step.10
  182.1 10.9 %all_to_all.67.data_ref = f32[4,2,16,640]{3,2,1,0:T(8,128)} all-to-all(f32[4,2,16,640]{3,2,1,0:T(8,128)} %x_step.10), channel_id=1, replica_groups=mesh['gx'=8,'gy'=4] {'gy'}, dimensions={0} | all-to-all | bytes 655360 | tf_op jit(solution)/shard_map/all_to_all | solution.py:340
  192.9 9.6 %y_step.5 = f32[4,2,16,640]{3,2,1,0:T(8,128)} custom-call(f32[4,2,16,640]{3,2,1,0:T(8,128)} %all_to_all.67.data_ref, f32[3,2,20,20,2,16,32]{6,5,4,3,2,1,0:T(8,128)} %w_ref.5, bf16[512,256]{1,0:T(8,128)(2,1)} %constant.41.clone.f_hi, bf16[512,256]{1,0:T(8,128)(2,1)} %constant.42.clone.f_lo, bf16[256,512]{1,0:T(8,128)(2,1)} %constant.43.clone.i_hi, ...), custom_call_target="tpu_custom_call" | custom-call | tf_op jit(solution)/shard_map/y_step/pallas_call | solution.py:249
  202.5 10.9 %all_to_all.68.data_ref = f32[4,2,16,640]{3,2,1,0:T(8,128)} all-to-all(f32[4,2,16,640]{3,2,1,0:T(8,128)} %y_step.5), channel_id=1, replica_groups=mesh['gx'=8,'gy'=4] {'gy'}, dimensions={0} | all-to-all | bytes 655360 | tf_op jit(solution)/shard_map/all_to_all | solution.py:342
  213.4 2.2 x_step.11
  215.6 15.2 %all_to_all.69 = f32[8,2,8,640]{3,2,1,0:T(8,128)} all-to-all(f32[8,2,8,640]{3,2,1,0:T(8,128)} %x_step.11), channel_id=1, replica_groups=mesh['gx'=8,'gy'=4] {'gx'}, dimensions={0} | all-to-all | bytes 655360 | tf_op jit(solution)/shard_map/all_to_all | solution.py:344
  230.8 8.2 %time_step.7 = f32[20,8,16,256]{3,2,1,0:T(8,128)} custom-call(f32[20,8,16,256]{3,2,1,0:T(8,128)} %get-tuple-element.11.refs_0_, f32[16,8,640]{2,1,0:T(8,128)} %bitcast.13, bf16[8,256,256]{2,1,0:T(8,128)(2,1)} %get-tuple-element.16.refs_2_, bf16[8,256,256]{2,1,0:T(8,128)(2,1)} %get-tuple-element.15.refs_3_, bf16[3,160,160]{2,1,0:T(8,128)(2,1)} %get-tuple-element.14.refs_4_, ...), custom_call_target="tpu_custom_call" | custom-call | tf_op jit(solution)/shard_map/time_step/pallas_call | solution.py:149
  (3 shorter events, 0.0 us)
Async XLA Ops:
  42.8 13.1 %copy-start.2 = (f32[3,20,20]{2,1,0:T(8,128)S(1)}, f32[3,20,20]{2,1,0:T(8,128)}, u32[]{:S(2)}) copy-start(f32[3,20,20]{2,1,0:T(8,128)} %param.16) | copy-start | bytes 14404
  52.5 10.1 %all-to-all-start.2 = ((f32[4,2,16,640]{3,2,1,0:T(8,128)}), f32[4,2,16,640]{3,2,1,0:T(8,128)S(1)}, u32[]{:S(2)}, u32[]{:S(2)}) async-start(f32[4,2,16,640]{3,2,1,0:T(8,128)} %y_step.3), calls=%async_computation.2 | async-start | bytes 655360 | tf_op jit(solution)/shard_map/all_to_all | solution.py:342
  62.6 0.7 copy-start.1
  65.6 13.6 %all-to-all-start.3 = ((f32[8,2,8,640]{3,2,1,0:T(8,128)}), f32[8,2,8,640]{3,2,1,0:T(8,128)S(1)}, u32[]{:S(2)}, u32[]{:S(2)}) async-start(f32[8,2,8,640]{3,2,1,0:T(8,128)} %x_step.7), calls=%async_computation.3 | async-start | bytes 655360 | tf_op jit(solution)/shard_map/all_to_all | solution.py:344
  72.0 4.1 %copy-start.3 = (f32[3,20]{1,0:T(4,128)S(1)}, f32[3,20]{1,0:T(4,128)}, u32[]{:S(2)}) copy-start(f32[3,20]{1,0:T(4,128)} %param.17) | copy-start | bytes 724
  79.2 0.9 copy-start
